TPU v7x, 128 devices: a whole 4x4x4 slice. The times are simulated.
128 devices in a mesh: slab: 64 (over y, z, x), blk: 2 (over core).
Axes of the slice: x: 4, y: 4, z: 4, core: 2. Of those that a mesh axis runs over, the one named last changes fastest.
Arguments:
- p_blocks: bfloat16 [2, 2048, 64, 64], P('blk', 'slab'), may hold values from -0.75 to 0.75
- basis_vals: bfloat16 [512, 8, 64, 128], P('slab'), may hold values from -0.75 to 0.75
- need_list: int32 [2, 64, 64, 4], P('blk', 'slab'), may hold values from 0 to 31, as said below
- tasks: int32 [2, 64, 4, 1536], P('blk', 'slab'), may hold values from 0 to 255, as said below
- task_counts: int32 [2, 64], P('blk', 'slab'), may hold values from 1 to 1536, as said below
Outputs:
- density: float32 [512, 128], P('slab')
- potential_blocks: float32 [2, 2048, 64, 64], P('blk', 'slab')
Inputs may be any that keep to these rules, and one draw needn't show every extreme that they name: The 4 entries of one need_list[c, s, o, :] are distinct. `tasks`: field 0 is below 8, fields 1 and 2 below 8, field 3 below 256. `task_counts`: some device has 1536 live tasks.
All inputs are finite; a program needn't handle non-finite values.
Results may differ from a plain program's by a relative error of at most 0.0029.
Values may be sent and summed in bfloat16 or wider, within the bound.
No kernel may reach another device: no remote copies, remote signals or barrier semaphores. Data moves between devices by JAX's collectives and lax.ppermute only.
A program may use at most 128 MiB of HBM per device.

v0:
```python
import jax
import jax.numpy as jnp
from jax import lax
from jax.sharding import PartitionSpec as P


def body(p_blocks, basis_vals, need_list, tasks, task_counts):
    slabs = lax.axis_size("slab")
    owned_blocks = p_blocks[0]
    blk_dev = owned_blocks.shape[0]
    block_size = owned_blocks.shape[1]
    wanted_ids = need_list[0, 0]
    capacity = wanted_ids.shape[1]
    requested = lax.all_to_all(wanted_ids, "slab", split_axis=0, concat_axis=0, tiled=True)
    column_all = lax.all_gather(owned_blocks, "slab", axis=0, tiled=True)
    offsets = jnp.arange(slabs, dtype=jnp.int32)[:, None] * blk_dev
    global_ids = (offsets + wanted_ids).reshape(-1)
    received = column_all[global_ids]
    task_fields = tasks[0, 0]
    live_count = task_counts[0, 0]
    nbat_local = basis_vals.shape[0]
    grid_coordinates = basis_vals.shape[3]
    task_slots = task_fields.shape[1]
    tile_rows = min(256, task_slots)
    tile_count = task_slots // tile_rows
    batch_range = jnp.arange(nbat_local, dtype=jnp.int32)

    def tile_terms(tile_index):
        fields_tile = lax.dynamic_slice_in_dim(task_fields, tile_index * tile_rows, tile_rows, 1)
        grid_batch_index = fields_tile[0]
        live_mask = (
            tile_index * tile_rows + jnp.arange(tile_rows, dtype=jnp.int32) < live_count
        ).astype(jnp.float32)
        left_vals = basis_vals[grid_batch_index, fields_tile[1]]
        right_side_values = basis_vals[grid_batch_index, fields_tile[2]]
        return (grid_batch_index, fields_tile[3], live_mask, left_vals, right_side_values)

    def density_tile(total, tile_index):
        grid_batch_index, slot_ids, live_mask, left_vals, right_side_values = tile_terms(tile_index)
        selected_entries = received[slot_ids]
        mapped_result = jnp.einsum(
            "zhf,zfx->zhx", selected_entries, right_side_values, preferred_element_type=jnp.float32
        )
        contrib = (
            jnp.sum(left_vals.astype(jnp.float32) * mapped_result, axis=1) * live_mask[:, None]
        )
        one_hot = (grid_batch_index[:, None] == batch_range[None, :]).astype(jnp.float32)
        added = jnp.dot(
            one_hot.T, contrib, precision=lax.Precision.HIGHEST, preferred_element_type=jnp.float32
        )
        return (total + added, None)

    tile_ids = jnp.arange(tile_count, dtype=jnp.int32)
    partial_density, _ = lax.scan(
        density_tile, jnp.zeros((nbat_local, grid_coordinates), jnp.float32), tile_ids
    )
    density = lax.psum(partial_density, "blk")
    potential = density / jnp.sqrt(1.0 + density * density)

    def potential_tile(slot_sums, tile_index):
        grid_batch_index, slot_ids, live_mask, left_vals, right_side_values = tile_terms(tile_index)
        weight_applied = (
            left_vals.astype(jnp.float32) * potential[grid_batch_index][:, None, :]
        ).astype(jnp.bfloat16)
        incomplete_sum_terms = jnp.einsum(
            "lkf,lgf->lkg", weight_applied, right_side_values, preferred_element_type=jnp.float32
        )
        incomplete_sum_terms = incomplete_sum_terms * live_mask[:, None, None]
        return (slot_sums.at[slot_ids].add(incomplete_sum_terms), None)

    slot_start = jnp.zeros((slabs * capacity, block_size, block_size), jnp.float32)
    slot_sums, _ = lax.scan(potential_tile, slot_start, tile_ids)
    returned = lax.all_to_all(
        slot_sums.reshape(slabs, capacity, block_size, block_size),
        "slab",
        split_axis=0,
        concat_axis=0,
        tiled=True,
    )
    owner_sums = jnp.zeros((blk_dev, block_size, block_size), jnp.float32)
    owner_sums = owner_sums.at[requested.reshape(-1)].add(
        returned.reshape(slabs * capacity, block_size, block_size)
    )
    return (density, owner_sums[None])


def solution(mesh):
    in_specs = (
        P("blk", "slab", None, None),
        P("slab", None, None, None),
        P("blk", "slab", None, None),
        P("blk", "slab", None, None),
        P("blk", "slab"),
    )
    out_specs = (P("slab", None), P("blk", "slab", None, None))
    return jax.shard_map(body, mesh=mesh, in_specs=in_specs, out_specs=out_specs, check_vma=False)
```

profile of v0, /device:TPU:0, one launch (start us, length us, event | category | flops | bytes accessed | tf_op | source)
XLA Modules:
  0.0 798.4 jit_solution(16260203998572006986)
XLA Ops:
  9.3 11.5 %all-to-all-start = ((s32[64,1,4]{2,1,0:T(1,128)}), s32[64,1,4]{2,1,0:T(1,128)S(1)}, u32[]{:S(2)}, u32[]{:S(2)}) async-start(s32[64,1,4]{2,1,0:T(1,128)} %bitcast.14), calls=%async_computation | async-start | bytes 65536 | tf_op jit(solution)/shard_map/all_to_all | solution.py:14
  21.9 152.0 %all-gather.3.cloned.1.call-done = bf16[1,2048,64,64]{3,2,0,1:T(8,128)(2,1)} async-done(((bf16[1,32,64,64]{3,2,0,1:T(8,128)(2,1)}), bf16[1,2048,64,64]{3,2,0,1:T(8,128)(2,1)}) %all-gather.3.cloned.1.call-update) | async-done | bytes 16777232 | tf_op jit(solution)/shard_map/all_gather | solution.py:15
  179.0 130.2 %while.22 = (s32[]{:T(128)}, f32[8,128]{1,0:T(8,128)S(1)}, s32[6]{0:T(128)S(1)}, s32[4,1536]{1,0:T(4,128)}, bf16[8,8,64,128]{3,2,1,0:T(8,128)(2,1)S(1)}, /*index...) while((s32[]{:T(128)}, f32[8,128]{1,0:T(8,128)S(1)}, ...), condition=%wide.region_2.3_spmd.clone, body=%wide.region_0.2_spmd.clone.sunk | while | flops 277883648 | bytes 31750408 | solution.py:54
  193.1 5.9 multiply_reduce_fusion.2
  279.9 5.9 multiply_reduce_fusion.2
  316.0 352.7 %while.21 = (s32[]{:T(128)}, f32[256,64,64]{2,1,0:T(8,128)}, s32[6]{0:T(128)S(1)}, s32[4,1536]{1,0:T(4,128)}, bf16[8,8,64,128]{3,2,1,0:T(8,128)(2,1)S(1)}, /*ind...) while((s32[]{:T(128)}, f32[256,64,64]{2,1,0:T(8,128)}, ...), condition=%wide.region_6.7_spmd, body=%wide.region_4.6_spmd.sunk | while | flops 276830976 | bytes 42358008 | solution.py:72
  326.3 9.0 %broadcast_multiply_fusion.2 = f32[256,64,64]{2,1,0:T(8,128)} fusion(f32[256]{0:T(256)S(1)} %compare_convert_fusion.4, bf16[256,64,128]{2,1,0:T(8,128)(2,1)} %gather_fusion, bf16[256,64,128]{2,1,0:T(8,128)(2,1)} %gather_fusion.1, f32[256,128]{1,0:T(8,128)S(1)} %gather_fusion.2), kind=kOutput, calls=%fused_computation.12.clone.1 | convolution fusion | flops 275775488 | bytes 12715008 | tf_op jit(solution)/shard_map/while/body/eval_jaxpr/lkf,lgf->lkg/dot_general | solution.py:65
  335.4 39.4 %scatter_fusion = f32[256,64,64]{2,1,0:T(8,128)} fusion(f32[256,64,64]{2,1,0:T(8,128)} %get-tuple-element.301, s32[256]{0:T(256)S(1)} %bitcast.104, f32[256,64,64]{2,1,0:T(8,128)} %broadcast_multiply_fusion.2), kind=kCustom, calls=%fused_computation.7.clone.1 | custom fusion | flops 1048576 | bytes 12583936 | tf_op jit(solution)/shard_map/while/body/eval_jaxpr/scatter-add | solution.py:69
  385.1 9.0 %broadcast_multiply_fusion.2 = f32[256,64,64]{2,1,0:T(8,128)} fusion(f32[256]{0:T(256)S(1)} %compare_convert_fusion.4, bf16[256,64,128]{2,1,0:T(8,128)(2,1)} %gather_fusion, bf16[256,64,128]{2,1,0:T(8,128)(2,1)} %gather_fusion.1, f32[256,128]{1,0:T(8,128)S(1)} %gather_fusion.2), kind=kOutput, calls=%fused_computation.12.clone.1 | convolution fusion | flops 275775488 | bytes 12715008 | tf_op jit(solution)/shard_map/while/body/eval_jaxpr/lkf,lgf->lkg/dot_general | solution.py:65
  394.1 39.5 %scatter_fusion = f32[256,64,64]{2,1,0:T(8,128)} fusion(f32[256,64,64]{2,1,0:T(8,128)} %get-tuple-element.301, s32[256]{0:T(256)S(1)} %bitcast.104, f32[256,64,64]{2,1,0:T(8,128)} %broadcast_multiply_fusion.2), kind=kCustom, calls=%fused_computation.7.clone.1 | custom fusion | flops 1048576 | bytes 12583936 | tf_op jit(solution)/shard_map/while/body/eval_jaxpr/scatter-add | solution.py:69
  443.9 9.0 %broadcast_multiply_fusion.2 = f32[256,64,64]{2,1,0:T(8,128)} fusion(f32[256]{0:T(256)S(1)} %compare_convert_fusion.4, bf16[256,64,128]{2,1,0:T(8,128)(2,1)} %gather_fusion, bf16[256,64,128]{2,1,0:T(8,128)(2,1)} %gather_fusion.1, f32[256,128]{1,0:T(8,128)S(1)} %gather_fusion.2), kind=kOutput, calls=%fused_computation.12.clone.1 | convolution fusion | flops 275775488 | bytes 12715008 | tf_op jit(solution)/shard_map/while/body/eval_jaxpr/lkf,lgf->lkg/dot_general | solution.py:65
  453.0 39.4 %scatter_fusion = f32[256,64,64]{2,1,0:T(8,128)} fusion(f32[256,64,64]{2,1,0:T(8,128)} %get-tuple-element.301, s32[256]{0:T(256)S(1)} %bitcast.104, f32[256,64,64]{2,1,0:T(8,128)} %broadcast_multiply_fusion.2), kind=kCustom, calls=%fused_computation.7.clone.1 | custom fusion | flops 1048576 | bytes 12583936 | tf_op jit(solution)/shard_map/while/body/eval_jaxpr/scatter-add | solution.py:69
  502.8 9.0 %broadcast_multiply_fusion.2 = f32[256,64,64]{2,1,0:T(8,128)} fusion(f32[256]{0:T(256)S(1)} %compare_convert_fusion.4, bf16[256,64,128]{2,1,0:T(8,128)(2,1)} %gather_fusion, bf16[256,64,128]{2,1,0:T(8,128)(2,1)} %gather_fusion.1, f32[256,128]{1,0:T(8,128)S(1)} %gather_fusion.2), kind=kOutput, calls=%fused_computation.12.clone.1 | convolution fusion | flops 275775488 | bytes 12715008 | tf_op jit(solution)/shard_map/while/body/eval_jaxpr/lkf,lgf->lkg/dot_general | solution.py:65
  511.8 39.3 %scatter_fusion = f32[256,64,64]{2,1,0:T(8,128)} fusion(f32[256,64,64]{2,1,0:T(8,128)} %get-tuple-element.301, s32[256]{0:T(256)S(1)} %bitcast.104, f32[256,64,64]{2,1,0:T(8,128)} %broadcast_multiply_fusion.2), kind=kCustom, calls=%fused_computation.7.clone.1 | custom fusion | flops 1048576 | bytes 12583936 | tf_op jit(solution)/shard_map/while/body/eval_jaxpr/scatter-add | solution.py:69
  561.4 9.0 %broadcast_multiply_fusion.2 = f32[256,64,64]{2,1,0:T(8,128)} fusion(f32[256]{0:T(256)S(1)} %compare_convert_fusion.4, bf16[256,64,128]{2,1,0:T(8,128)(2,1)} %gather_fusion, bf16[256,64,128]{2,1,0:T(8,128)(2,1)} %gather_fusion.1, f32[256,128]{1,0:T(8,128)S(1)} %gather_fusion.2), kind=kOutput, calls=%fused_computation.12.clone.1 | convolution fusion | flops 275775488 | bytes 12715008 | tf_op jit(solution)/shard_map/while/body/eval_jaxpr/lkf,lgf->lkg/dot_general | solution.py:65
  570.5 39.4 %scatter_fusion = f32[256,64,64]{2,1,0:T(8,128)} fusion(f32[256,64,64]{2,1,0:T(8,128)} %get-tuple-element.301, s32[256]{0:T(256)S(1)} %bitcast.104, f32[256,64,64]{2,1,0:T(8,128)} %broadcast_multiply_fusion.2), kind=kCustom, calls=%fused_computation.7.clone.1 | custom fusion | flops 1048576 | bytes 12583936 | tf_op jit(solution)/shard_map/while/body/eval_jaxpr/scatter-add | solution.py:69
  620.2 9.0 %broadcast_multiply_fusion.2 = f32[256,64,64]{2,1,0:T(8,128)} fusion(f32[256]{0:T(256)S(1)} %compare_convert_fusion.4, bf16[256,64,128]{2,1,0:T(8,128)(2,1)} %gather_fusion, bf16[256,64,128]{2,1,0:T(8,128)(2,1)} %gather_fusion.1, f32[256,128]{1,0:T(8,128)S(1)} %gather_fusion.2), kind=kOutput, calls=%fused_computation.12.clone.1 | convolution fusion | flops 275775488 | bytes 12715008 | tf_op jit(solution)/shard_map/while/body/eval_jaxpr/lkf,lgf->lkg/dot_general | solution.py:65
  629.2 39.5 %scatter_fusion = f32[256,64,64]{2,1,0:T(8,128)} fusion(f32[256,64,64]{2,1,0:T(8,128)} %get-tuple-element.301, s32[256]{0:T(256)S(1)} %bitcast.104, f32[256,64,64]{2,1,0:T(8,128)} %broadcast_multiply_fusion.2), kind=kCustom, calls=%fused_computation.7.clone.1 | custom fusion | flops 1048576 | bytes 12583936 | tf_op jit(solution)/shard_map/while/body/eval_jaxpr/scatter-add | solution.py:69
  668.7 9.7 %reshape.408 = f32[64,1,16384]{2,1,0:T(1,128)} reshape(f32[64,4,64,64]{3,2,1,0:T(8,128)} %bitcast.99) | data formatting | bytes 8388608
  678.4 9.1 %all-to-all-start.1 = ((f32[64,1,16384]{2,1,0:T(1,128)}), f32[64,1,16384]{2,1,0:T(1,128)}, u32[]{:S(2)}, u32[]{:S(2)}) async-start(f32[64,1,16384]{2,1,0:T(1,128)} %reshape.408), calls=%async_computation.1 | async-start | bytes 8388608 | tf_op jit(solution)/shard_map/all_to_all | solution.py:73
  688.9 53.8 %all-to-all-done.1 = f32[64,1,16384]{2,1,0:T(1,128)} async-done(((f32[64,1,16384]{2,1,0:T(1,128)}), f32[64,1,16384]{2,1,0:T(1,128)}, u32[]{:S(2)}, u32[]{:S(2)}) %all-to-all-start.1) | async-done | bytes 4194336 | tf_op jit(solution)/shard_map/all_to_all | solution.py:73
  743.2 13.7 %reduce.4 = f32[64,16384]{1,0:T(8,128)} reduce(f32[64,1,16384]{2,1,0:T(1,128)} %all-to-all-done.1, f32[]{:T(128)} %broadcast.330), dimensions={1}, to_apply=%all_to_all.11.reduce_sub_computation | reduce | bytes 8388612 | tf_op jit(solution)/shard_map/all_to_all | solution.py:73
  757.0 7.4 reshape.409
  764.4 26.1 %scatter_fusion.1 = f32[32,64,64]{2,1,0:T(8,128)S(1)} fusion(f32[32,64,64]{2,1,0:T(8,128)S(1)} %broadcast_in_dim.9, s32[256]{0:T(256)S(1)} %bitcast.109, f32[256,64,64]{2,1,0:T(8,128)} %bitcast.101), kind=kCustom, calls=%fused_computation.8 | custom fusion | flops 1048576 | bytes 12583936 | tf_op jit(solution)/shard_map/scatter-add | solution.py:81
  (129 shorter events, 190.3 us)
Async XLA Ops:
  7.2 166.8 %all-gather.3.cloned.1.call-start = ((), (), s32[]{:S(2)}) async-start(), calls=%async_computation.2 | async-start | bytes 34078720 | tf_op jit(solution)/shard_map/all_gather | solution.py:15
  9.3 669.1 %all-to-all-start = ((s32[64,1,4]{2,1,0:T(1,128)}), s32[64,1,4]{2,1,0:T(1,128)S(1)}, u32[]{:S(2)}, u32[]{:S(2)}) async-start(s32[64,1,4]{2,1,0:T(1,128)} %bitcast.14), calls=%async_computation | async-start | bytes 65536 | tf_op jit(solution)/shard_map/all_to_all | solution.py:14
  174.0 5.0 copy-start
  311.7 4.3 copy-start.2
  678.4 64.3 %all-to-all-start.1 = ((f32[64,1,16384]{2,1,0:T(1,128)}), f32[64,1,16384]{2,1,0:T(1,128)}, u32[]{:S(2)}, u32[]{:S(2)}) async-start(f32[64,1,16384]{2,1,0:T(1,128)} %reshape.408), calls=%async_computation.1 | async-start | bytes 8388608 | tf_op jit(solution)/shard_map/all_to_all | solution.py:73
  790.6 1.0 copy-start.1
Sparse Core Ops, SparseCore 0:
  10.9 163.0 all-gather.2
where the time goes:
time: 804 us; the launch traced here: 798 us
  other arithmetic  296 us (37%)
  waiting for transfers between devices  207 us (26%)
  local copies, waits for them, and re-layouts  159 us (20%)
  matrix products  91.6 us (11%)
  starting transfers between devices  20.7 us (3%)
  between operations  14.1 us (2%)
  loops' own time  8.14 us (1%)
    scatter-add x6, other arithmetic, potential_tile(): return (slot_sums.at[slot_ids].add(incomplete_sum_terms), None)  237 us
    all_gather x1, waiting for transfers between devices, body(): column_all = lax.all_gather(owned_blocks, 'slab', axis=0, tiled=True)  152 us
    dot_general x6, matrix products, potential_tile(): jnp.einsum('lkf,lgf->lkg', weight_applied, right_side_values, preferred_e...  54.1 us
    all_to_all x1, waiting for transfers between devices, body(): lax.all_to_all(slot_sums.reshape(slabs, capacity, block_size, block_size)...  53.8 us
    gather x12, local copies, waits for them, and re-layouts, tile_terms(): right_side_values = basis_vals[grid_batch_index, fields_tile[2]]  40 us
    gather x12, local copies, waits for them, and re-layouts, tile_terms(): left_vals = basis_vals[grid_batch_index, fields_tile[1]]  40 us
    dot_general x6, matrix products, density_tile(): jnp.einsum('zhf,zfx->zhx', selected_entries, right_side_values, preferred...  35.5 us
    gather x6, local copies, waits for them, and re-layouts, density_tile(): selected_entries = received[slot_ids]  31.5 us
  transfers between devices with their start and end apart: 3, of which 2 were waited for; matrix products, arithmetic and copies ran while one was open for 62% of the time, Pallas kernels for 0%

commit v1 on v0

--- a/solution.py
+++ b/solution.py
@@ -2,6 +2,13 @@
 import jax.numpy as jnp
 from jax import lax
 from jax.sharding import PartitionSpec as P
+
+
+def form_node(frame_in, axis_key):
+    frame_out = jax.lax.axis_size(axis_key)
+    res = jnp.stack([frame_in] * frame_out, axis=0)
+    spare = jax.lax.all_to_all(res, axis_key, 0, 0)
+    return jnp.concatenate(spare, axis=0)
 
 
 def body(p_blocks, basis_vals, need_list, tasks, task_counts):
@@ -12,7 +19,7 @@
     wanted_ids = need_list[0, 0]
     capacity = wanted_ids.shape[1]
     requested = lax.all_to_all(wanted_ids, "slab", split_axis=0, concat_axis=0, tiled=True)
-    column_all = lax.all_gather(owned_blocks, "slab", axis=0, tiled=True)
+    column_all = form_node(owned_blocks, "slab")
     offsets = jnp.arange(slabs, dtype=jnp.int32)[:, None] * blk_dev
     global_ids = (offsets + wanted_ids).reshape(-1)
     received = column_all[global_ids]

time: 804 us -> 1050 us (1.31)
  local copies, waits for them, and re-layouts: 159 us -> 273 us
  waiting for transfers between devices: 207 us -> 308 us
  starting transfers between devices: 20.7 us -> 63.7 us
  between operations: 14.1 us -> 0.75 us
    all_to_all x0 -> x1, waiting for transfers between devices: none -> 255 us  [form_node(): spare = jax.lax.all_to_all(res, axis_key, 0, 0)]
    all_gather x1 -> x0, waiting for transfers between devices: 152 us -> none  [body(): column_all = lax.all_gather(owned_blocks, 'slab', axis=0, tiled=True)]
    unnamed x9 -> x13, local copies, waits for them, and re-layouts: 19.4 us -> 122 us
    all_to_all x1, starting transfers between devices: 11.5 us -> 41.1 us  [body(): lax.all_to_all(wanted_ids, 'slab', split_axis=0, concat_axis=0, tiled=True)]
    another operation x0 -> x1, local copies, waits for them, and re-layouts: none -> 12 us  [form_node(): res = jnp.stack([frame_in] * frame_out, axis=0)]
    all_to_all x0 -> x1, starting transfers between devices: none -> 11.9 us  [form_node(): spare = jax.lax.all_to_all(res, axis_key, 0, 0)]
  transfers between devices with their start and end apart: 3 -> 3, of which waited for: 2 -> 2; matrix products, arithmetic and copies ran while one was open for 62% -> 53% of each run, Pallas kernels for 0% -> 0%
where the time goes in v1:
time: 1050 us; the launch traced here: 1040 us
  waiting for transfers between devices  308 us (29%)
  other arithmetic  297 us (28%)
  local copies, waits for them, and re-layouts  273 us (26%)
  matrix products  91.6 us (9%)
  starting transfers between devices  63.7 us (6%)
    all_to_all x1, waiting for transfers between devices, form_node(): spare = jax.lax.all_to_all(res, axis_key, 0, 0)  255 us
    scatter-add x6, other arithmetic, potential_tile(): return (slot_sums.at[slot_ids].add(incomplete_sum_terms), None)  237 us
    unnamed x13, local copies, waits for them, and re-layouts  122 us
    dot_general x6, matrix products, potential_tile(): jnp.einsum('lkf,lgf->lkg', weight_applied, right_side_values, preferred_e...  54.1 us
    all_to_all x1, waiting for transfers between devices, body(): lax.all_to_all(slot_sums.reshape(slabs, capacity, block_size, block_size)...  53.1 us
    all_to_all x1, starting transfers between devices, body(): lax.all_to_all(wanted_ids, 'slab', split_axis=0, concat_axis=0, tiled=True)  41.1 us
    gather x12, local copies, waits for them, and re-layouts, tile_terms(): right_side_values = basis_vals[grid_batch_index, fields_tile[2]]  40 us
    gather x12, local copies, waits for them, and re-layouts, tile_terms(): left_vals = basis_vals[grid_batch_index, fields_tile[1]]  40 us
  transfers between devices with their start and end apart: 3, of which 2 were waited for; matrix products, arithmetic and copies ran while one was open for 53% of the time, Pallas kernels for 0%

profile of v1, /device:TPU:0, one launch (start us, length us, event | category | flops | bytes accessed | tf_op | source)
XLA Modules:
  0.0 1044.2 jit_solution(17983553166799614649)
XLA Ops:
  0.6 12.0 %stack.3 = bf16[64,32,64,64]{3,2,1,0:T(8,128)(2,1)} broadcast(bf16[32,64,64]{2,1,0:T(8,128)(2,1)} %bitcast.103), dimensions={1,2,3} | broadcast | bytes 17039360 | tf_op jit(solution)/shard_map/stack | solution.py:9
  12.6 52.2 %reshape.412 = bf16[64,2,65536]{2,1,0:T(2,128)(2,1)} reshape(bf16[64,32,64,64]{3,2,1,0:T(8,128)(2,1)} %stack.3) | data formatting | bytes 33554432
  64.8 11.9 %all-to-all-start = ((bf16[64,2,65536]{2,1,0:T(2,128)(2,1)}), bf16[64,2,65536]{2,1,0:T(2,128)(2,1)}, u32[]{:S(2)}, u32[]{:S(2)}) async-start(bf16[64,2,65536]{2,1,0:T(2,128)(2,1)} %reshape.412), calls=%async_computation | async-start | bytes 33554432 | tf_op jit(solution)/shard_map/all_to_all | solution.py:10
  78.5 254.6 %all-to-all-done = bf16[64,2,65536]{2,1,0:T(2,128)(2,1)} async-done(((bf16[64,2,65536]{2,1,0:T(2,128)(2,1)}), bf16[64,2,65536]{2,1,0:T(2,128)(2,1)}, u32[]{:S(2)}, u32[]{:S(2)}) %all-to-all-start) | async-done | bytes 16777248 | tf_op jit(solution)/shard_map/all_to_all | solution.py:10
  333.1 41.1 %all-to-all-start.1 = ((s32[64,1,4]{2,1,0:T(1,128)}), s32[64,1,4]{2,1,0:T(1,128)}, u32[]{:S(2)}, u32[]{:S(2)}) async-start(s32[64,1,4]{2,1,0:T(1,128)} %bitcast.14), calls=%async_computation.1 | async-start | bytes 65536 | tf_op jit(solution)/shard_map/all_to_all | solution.py:21
  374.2 50.7 %reshape.413 = bf16[64,32,64,64]{3,2,1,0:T(8,128)(2,1)} reshape(bf16[64,2,65536]{2,1,0:T(2,128)(2,1)} %all-to-all-done) | data formatting | bytes 33554432
  430.0 130.2 %while.22 = (s32[]{:T(128)}, f32[8,128]{1,0:T(8,128)S(1)}, s32[6]{0:T(128)S(1)}, s32[4,1536]{1,0:T(4,128)}, bf16[8,8,64,128]{3,2,1,0:T(8,128)(2,1)S(1)}, /*index...) while((s32[]{:T(128)}, f32[8,128]{1,0:T(8,128)S(1)}, ...), condition=%wide.region_2.3_spmd.clone, body=%wide.region_0.2_spmd.clone.sunk | while | flops 277883648 | bytes 31750416 | solution.py:61
  567.0 352.7 %while.21 = (s32[]{:T(128)}, f32[256,64,64]{2,1,0:T(8,128)}, s32[6]{0:T(128)S(1)}, s32[4,1536]{1,0:T(4,128)}, bf16[8,8,64,128]{3,2,1,0:T(8,128)(2,1)S(1)}, /*ind...) while((s32[]{:T(128)}, f32[256,64,64]{2,1,0:T(8,128)}, ...), condition=%wide.region_6.7_spmd, body=%wide.region_4.6_spmd.sunk | while | flops 276830976 | bytes 42358016 | solution.py:79
  577.3 9.0 broadcast_multiply_fusion.2
  586.3 39.4 %scatter_fusion = f32[256,64,64]{2,1,0:T(8,128)} fusion(f32[256,64,64]{2,1,0:T(8,128)} %get-tuple-element.308, s32[256]{0:T(256)S(1)} %bitcast.104, f32[256,64,64]{2,1,0:T(8,128)} %broadcast_multiply_fusion.2), kind=kCustom, calls=%fused_computation.7.clone.1 | custom fusion | flops 1048576 | bytes 12583936 | tf_op jit(solution)/shard_map/while/body/eval_jaxpr/scatter-add | solution.py:76
  636.1 9.0 broadcast_multiply_fusion.2
  645.1 39.5 %scatter_fusion = f32[256,64,64]{2,1,0:T(8,128)} fusion(f32[256,64,64]{2,1,0:T(8,128)} %get-tuple-element.308, s32[256]{0:T(256)S(1)} %bitcast.104, f32[256,64,64]{2,1,0:T(8,128)} %broadcast_multiply_fusion.2), kind=kCustom, calls=%fused_computation.7.clone.1 | custom fusion | flops 1048576 | bytes 12583936 | tf_op jit(solution)/shard_map/while/body/eval_jaxpr/scatter-add | solution.py:76
  694.9 9.0 broadcast_multiply_fusion.2
  703.9 39.4 %scatter_fusion = f32[256,64,64]{2,1,0:T(8,128)} fusion(f32[256,64,64]{2,1,0:T(8,128)} %get-tuple-element.308, s32[256]{0:T(256)S(1)} %bitcast.104, f32[256,64,64]{2,1,0:T(8,128)} %broadcast_multiply_fusion.2), kind=kCustom, calls=%fused_computation.7.clone.1 | custom fusion | flops 1048576 | bytes 12583936 | tf_op jit(solution)/shard_map/while/body/eval_jaxpr/scatter-add | solution.py:76
  753.7 9.0 broadcast_multiply_fusion.2
  762.8 39.3 %scatter_fusion = f32[256,64,64]{2,1,0:T(8,128)} fusion(f32[256,64,64]{2,1,0:T(8,128)} %get-tuple-element.308, s32[256]{0:T(256)S(1)} %bitcast.104, f32[256,64,64]{2,1,0:T(8,128)} %broadcast_multiply_fusion.2), kind=kCustom, calls=%fused_computation.7.clone.1 | custom fusion | flops 1048576 | bytes 12583936 | tf_op jit(solution)/shard_map/while/body/eval_jaxpr/scatter-add | solution.py:76
  821.4 39.4 %scatter_fusion = f32[256,64,64]{2,1,0:T(8,128)} fusion(f32[256,64,64]{2,1,0:T(8,128)} %get-tuple-element.308, s32[256]{0:T(256)S(1)} %bitcast.104, f32[256,64,64]{2,1,0:T(8,128)} %broadcast_multiply_fusion.2), kind=kCustom, calls=%fused_computation.7.clone.1 | custom fusion | flops 1048576 | bytes 12583936 | tf_op jit(solution)/shard_map/while/body/eval_jaxpr/scatter-add | solution.py:76
  871.2 9.0 broadcast_multiply_fusion.2
  880.2 39.5 %scatter_fusion = f32[256,64,64]{2,1,0:T(8,128)} fusion(f32[256,64,64]{2,1,0:T(8,128)} %get-tuple-element.308, s32[256]{0:T(256)S(1)} %bitcast.104, f32[256,64,64]{2,1,0:T(8,128)} %broadcast_multiply_fusion.2), kind=kCustom, calls=%fused_computation.7.clone.1 | custom fusion | flops 1048576 | bytes 12583936 | tf_op jit(solution)/shard_map/while/body/eval_jaxpr/scatter-add | solution.py:76
  919.7 9.7 reshape.414
  929.4 10.8 %all-to-all-start.2 = ((f32[64,1,16384]{2,1,0:T(1,128)}), f32[64,1,16384]{2,1,0:T(1,128)}, u32[]{:S(2)}, u32[]{:S(2)}) async-start(f32[64,1,16384]{2,1,0:T(1,128)} %reshape.414), calls=%async_computation.2 | async-start | bytes 8388608 | tf_op jit(solution)/shard_map/all_to_all | solution.py:80
  942.3 53.1 %all-to-all-done.2 = f32[64,1,16384]{2,1,0:T(1,128)} async-done(((f32[64,1,16384]{2,1,0:T(1,128)}), f32[64,1,16384]{2,1,0:T(1,128)}, u32[]{:S(2)}, u32[]{:S(2)}) %all-to-all-start.2) | async-done | bytes 4194336 | tf_op jit(solution)/shard_map/all_to_all | solution.py:80
  995.9 13.7 %reduce.4 = f32[64,16384]{1,0:T(8,128)} reduce(f32[64,1,16384]{2,1,0:T(1,128)} %all-to-all-done.2, f32[]{:T(128)} %broadcast.331), dimensions={1}, to_apply=%all_to_all.15.reduce_sub_computation | reduce | bytes 8388612 | tf_op jit(solution)/shard_map/all_to_all | solution.py:80
  1017.1 26.1 %scatter_fusion.1 = f32[32,64,64]{2,1,0:T(8,128)S(1)} fusion(f32[32,64,64]{2,1,0:T(8,128)S(1)} %broadcast_in_dim.9, s32[256]{0:T(256)S(1)} %bitcast.109, f32[256,64,64]{2,1,0:T(8,128)} %bitcast.102), kind=kCustom, calls=%fused_computation.8 | custom fusion | flops 1048576 | bytes 12583936 | tf_op jit(solution)/shard_map/scatter-add | solution.py:88
  (133 shorter events, 217.7 us)
Async XLA Ops:
  64.8 12.1 %copy-start.3 = (s32[1,1,64,4]{2,3,1,0:T(4,128)S(1)}, s32[1,1,64,4]{2,3,1,0:T(4,128)}, u32[]{:S(2)}) copy-start(s32[1,1,64,4]{2,3,1,0:T(4,128)} %param.11) | copy-start | bytes 3076
  64.8 268.3 %all-to-all-start = ((bf16[64,2,65536]{2,1,0:T(2,128)(2,1)}), bf16[64,2,65536]{2,1,0:T(2,128)(2,1)}, u32[]{:S(2)}, u32[]{:S(2)}) async-start(bf16[64,2,65536]{2,1,0:T(2,128)(2,1)} %reshape.412), calls=%async_computation | async-start | bytes 33554432 | tf_op jit(solution)/shard_map/all_to_all | solution.py:10
  333.1 596.3 %all-to-all-start.1 = ((s32[64,1,4]{2,1,0:T(1,128)}), s32[64,1,4]{2,1,0:T(1,128)}, u32[]{:S(2)}, u32[]{:S(2)}) async-start(s32[64,1,4]{2,1,0:T(1,128)} %bitcast.14), calls=%async_computation.1 | async-start | bytes 65536 | tf_op jit(solution)/shard_map/all_to_all | solution.py:21
  424.9 5.0 copy-start
  562.7 4.3 copy-start.2
  929.4 66.0 %all-to-all-start.2 = ((f32[64,1,16384]{2,1,0:T(1,128)}), f32[64,1,16384]{2,1,0:T(1,128)}, u32[]{:S(2)}, u32[]{:S(2)}) async-start(f32[64,1,16384]{2,1,0:T(1,128)} %reshape.414), calls=%async_computation.2 | async-start | bytes 8388608 | tf_op jit(solution)/shard_map/all_to_all | solution.py:80
  1043.3 1.0 copy-start.1
